TPU v7x, 32 devices: a whole 2x2x4 slice. The times are simulated.
32 devices in a mesh: tok: 8 (over y, x, core), mdl: 4 (over z).
Axes of the slice: x: 2, y: 2, z: 4, core: 2. Of those that a mesh axis runs over, the one named last changes fastest.
Arguments:
- hidden_states: bfloat16 [4096, 3072], P('tok', 'mdl'), may hold values from -36 to 36
- lengths: int32 [2], replicated, may hold values from 1 to 2277, 3644 in all
- positions: int32 [3, 4096], P(None, 'tok'), may hold values from 0 to 44, as said below
- modulation: float32 [6, 3072], replicated, may hold values from -3 to 3
- query_weight: bfloat16 [3072, 3072], P('tok', 'mdl'), may hold values from -1.1 to 1.1
- key_weight: bfloat16 [3072, 3072], P('tok', 'mdl'), may hold values from -1.1 to 1.1
- value_weight: bfloat16 [3072, 3072], P('tok', 'mdl'), may hold values from -0.109375 to 0.109375
- out_weight: bfloat16 [3072, 3072], P('tok', 'mdl'), may hold values from -0.109375 to 0.109375
- query_gain: float32 [64], replicated, may hold values from 0.1 to 1.9
- key_gain: float32 [64], replicated, may hold values from 0.1 to 1.9
Outputs:
- updated: bfloat16 [4096, 3072], P('tok', 'mdl')
Inputs may be any that keep to these rules, and one draw needn't show every extreme that they name: lengths[0] + lengths[1] = 3644, and neither of them exceeds 2277. `positions`: frame below 13, row below 30, column below 45.
All inputs are finite; a program needn't handle non-finite values.
Results may differ from a plain program's by a relative error of at most 0.0045.
Values may be sent and summed in bfloat16 or wider, within the bound.
A program may use at most 128 MiB of HBM per device.

v0:
```python
import jax
import jax.numpy as jnp
from jax import lax
from jax.sharding import PartitionSpec as P

TEXT = 226


def token_labels(row_index, lengths):
    bound = TEXT + lengths[0]
    request = (row_index >= bound).astype(jnp.int32)
    place = row_index - request * bound
    return (request, place < TEXT, bound)


def modulate(rows_bf, modulation, is_text):
    values = rows_bf.astype(jnp.float32)
    center = values - jnp.mean(values, axis=1, keepdims=True)
    spread = jnp.mean(center * center, axis=1, keepdims=True)
    normal = center * lax.rsqrt(spread + 1e-05)
    textual = is_text[:, None]
    shift = jnp.where(textual, modulation[3][None, :], modulation[0][None, :])
    scale = jnp.where(textual, modulation[4][None, :], modulation[1][None, :])
    return (normal * (1.0 + scale) + shift).astype(jnp.bfloat16)


def pair_angles(positions, pairs):
    index = jnp.arange(pairs, dtype=jnp.int32)
    first = pairs // 4
    second = (pairs - first) // 2
    third = pairs - first - second
    component = jnp.where(index < first, 0, jnp.where(index < first + second, 1, 2))
    local = index - jnp.where(component == 0, 0, jnp.where(component == 1, first, first + second))
    count = jnp.where(component == 0, first, jnp.where(component == 1, second, third))
    rates = jnp.power(jnp.float32(10000.0), -local.astype(jnp.float32) / count.astype(jnp.float32))
    places = positions.astype(jnp.float32)
    chosen = jnp.where(
        component[:, None] == 0,
        places[0][None, :],
        jnp.where(component[:, None] == 1, places[1][None, :], places[2][None, :]),
    )
    return jnp.transpose(chosen * rates[:, None])


def head_norm(projected, gain, angles, is_text):
    width = gain.shape[0]
    shaped = projected.reshape(projected.shape[0], -1, width)
    center = shaped - jnp.mean(shaped, axis=2, keepdims=True)
    spread = jnp.mean(center * center, axis=2, keepdims=True)
    normal = center * lax.rsqrt(spread + 1e-06) * gain
    half = width // 2
    cosine = jnp.cos(angles)[:, None, :]
    sine = jnp.sin(angles)[:, None, :]
    lower = normal[:, :, :half]
    upper = normal[:, :, half:]
    turned = jnp.concatenate([lower * cosine - upper * sine, lower * sine + upper * cosine], axis=2)
    return jnp.where(is_text[:, None, None], normal, turned).astype(jnp.bfloat16)


def shards(
    hidden_states,
    lengths,
    positions,
    modulation,
    query_weight,
    key_weight,
    value_weight,
    out_weight,
    query_gain,
    key_gain,
):
    own_rows = hidden_states.shape[0]
    local_width = query_weight.shape[1]
    head_width = query_gain.shape[0]
    local_heads = local_width // head_width
    full_rows = lax.all_gather(hidden_states, "mdl", axis=1, tiled=True)
    row_index = lax.axis_index("tok") * own_rows + jnp.arange(own_rows, dtype=jnp.int32)
    request, is_text, bound = token_labels(row_index, lengths)
    normed = modulate(full_rows, modulation, is_text)
    angles = pair_angles(positions, head_width // 2)
    pieces = (
        lax.all_gather(query_weight, "tok", axis=0, tiled=True),
        lax.all_gather(key_weight, "tok", axis=0, tiled=True),
        lax.all_gather(value_weight, "tok", axis=0, tiled=True),
    )
    columns = normed
    query_sum, key_sum, value_sum = tuple(
        (
            jnp.dot(columns, pieces[number], preferred_element_type=jnp.float32)
            for number in range(3)
        )
    )
    query = head_norm(query_sum, query_gain, angles, is_text)
    key_flat = head_norm(key_sum, key_gain, angles, is_text).reshape(own_rows, local_width)
    value_flat = value_sum.astype(jnp.bfloat16)
    factor = head_width ** (-0.5)

    def block_terms(block_keys, block_values, block_start):
        size = block_keys.shape[0]
        key_request = (block_start + jnp.arange(size, dtype=jnp.int32) >= bound).astype(jnp.int32)
        score = (
            jnp.einsum(
                "qhd,khd->hqk",
                query,
                block_keys.reshape(size, local_heads, head_width),
                preferred_element_type=jnp.float32,
            )
            * factor
        )
        same = (request[:, None] == key_request[None, :])[None, :, :]
        expo = jnp.where(same, jnp.exp(score), jnp.float32(0.0))
        totals = jnp.transpose(jnp.sum(expo, axis=2))
        weighted = jnp.einsum(
            "hqk,khd->qhd",
            expo.astype(jnp.bfloat16),
            block_values.reshape(size, local_heads, head_width),
            preferred_element_type=jnp.float32,
        )
        return (weighted.reshape(own_rows, local_width), totals)

    initial = (
        jnp.zeros((own_rows, local_width), jnp.float32),
        jnp.zeros((own_rows, local_heads), jnp.float32),
    )
    keys_piece = lax.all_gather(key_flat, "tok", axis=0, tiled=True)
    values_piece = lax.all_gather(value_flat, "tok", axis=0, tiled=True)
    count = keys_piece.shape[0]
    block = 1024
    steps_count = count // block

    def step_block(inner, operands):
        block_keys, block_values, offset = operands
        weighted, totals = block_terms(block_keys, block_values, offset)
        return ((inner[0] + weighted, inner[1] + totals), None)

    offsets = jnp.arange(steps_count, dtype=jnp.int32) * block
    result, unused = lax.scan(
        step_block,
        initial,
        (
            keys_piece.reshape(steps_count, block, local_width),
            values_piece.reshape(steps_count, block, local_width),
            offsets,
        ),
    )
    weighted, totals = result
    attended = (
        (weighted.reshape(own_rows, local_heads, head_width) / totals[:, :, None])
        .reshape(own_rows, local_width)
        .astype(jnp.bfloat16)
    )
    all_heads = lax.all_gather(attended, "mdl", axis=1, tiled=True)
    out_width = out_weight.shape[1]
    columns = all_heads
    projected = jnp.dot(
        columns,
        lax.all_gather(out_weight, "tok", axis=0, tiled=True),
        preferred_element_type=jnp.float32,
    )
    gate_rows = lax.dynamic_slice_in_dim(
        modulation, lax.axis_index("mdl") * out_width, out_width, 1
    )
    gate = jnp.where(is_text[:, None], gate_rows[5][None, :], gate_rows[2][None, :])
    return (hidden_states.astype(jnp.float32) + gate * projected).astype(jnp.bfloat16)


def solution(mesh):
    return jax.shard_map(
        shards,
        mesh=mesh,
        in_specs=(
            P("tok", "mdl"),
            P(),
            P(None, "tok"),
            P(),
            P("tok", "mdl"),
            P("tok", "mdl"),
            P("tok", "mdl"),
            P("tok", "mdl"),
            P(),
            P(),
        ),
        out_specs=P("tok", "mdl"),
        check_vma=False,
    )
```

profile of v0, /device:TPU:0, one launch (start us, length us, event | category | flops | bytes accessed | tf_op | source)
XLA Modules:
  0.0 505.0 jit_solution(1737966056882740450)
XLA Ops:
  10.6 64.5 %all-gather.9.cloned.1.call-done = bf16[512,3072]{1,0:T(8,128)(2,1)} async-done(((bf16[512,768]{1,0:T(8,128)(2,1)}), bf16[512,3072]{1,0:T(8,128)(2,1)}) %all-gather.9.cloned.1.call-update) | async-done | bytes 3145744 | tf_op jit(solution)/shard_map/all_gather | solution.py:76
  75.1 2.5 convert_reduce_fusion
  78.9 3.7 fusion.16
  82.7 32.0 %all-gather.15.cloned.1.call-done = bf16[3072,768]{1,0:T(8,128)(2,1)} async-done(((bf16[384,768]{1,0:T(8,128)(2,1)}), bf16[3072,768]{1,0:T(8,128)(2,1)}) %all-gather.15.cloned.1.call-update) | async-done | bytes 4718608 | tf_op jit(solution)/shard_map/all_gather | solution.py:83
  114.7 5.9 %fusion.25 = f32[512,768]{1,0:T(8,128)S(1)} fusion(bf16[512,3072]{1,0:T(8,128)(2,1)} %fusion.16, bf16[3072,768]{1,0:T(8,128)(2,1)} %all-gather.15.cloned.1.call-done), kind=kOutput, calls=%fused_computation.64 | convolution fusion | flops 2415919104 | bytes 9437184 | tf_op jit(solution)/shard_map/dot_general | solution.py:89
  121.9 33.6 %all-gather.19.cloned.1.call-done = bf16[3072,768]{1,0:T(8,128)(2,1)} async-done(((bf16[384,768]{1,0:T(8,128)(2,1)}), bf16[3072,768]{1,0:T(8,128)(2,1)}) %all-gather.19.cloned.1.call-update) | async-done | bytes 4718608 | tf_op jit(solution)/shard_map/all_gather | solution.py:82
  155.5 5.5 %fusion.26 = f32[512,768]{0,1:T(8,128)S(1)} fusion(bf16[512,3072]{1,0:T(8,128)(2,1)} %fusion.16, bf16[3072,768]{1,0:T(8,128)(2,1)} %all-gather.19.cloned.1.call-done), kind=kOutput, calls=%fused_computation.65 | convolution fusion | flops 2415919104 | bytes 9437184 | tf_op jit(solution)/shard_map/dot_general | solution.py:89
  171.1 3.8 select_convert_fusion
  175.1 21.0 %all-gather.11.cloned.1.call-done = bf16[3072,768]{1,0:T(8,128)(2,1)} async-done(((bf16[384,768]{1,0:T(8,128)(2,1)}), bf16[3072,768]{1,0:T(8,128)(2,1)}) %all-gather.11.cloned.1.call-update) | async-done | bytes 4718608 | tf_op jit(solution)/shard_map/all_gather | solution.py:84
  196.2 6.8 %convolution_convert_fusion = bf16[512,768]{1,0:T(8,128)(2,1)} fusion(bf16[512,3072]{1,0:T(8,128)(2,1)} %fusion.16, bf16[3072,768]{1,0:T(8,128)(2,1)} %all-gather.11.cloned.1.call-done), kind=kOutput, calls=%fused_computation.36 | convolution fusion | flops 2416312320 | bytes 8650752 | tf_op jit(solution)/shard_map/dot_general | solution.py:89
  205.3 38.2 %all-gather.17.cloned.1.call-done = bf16[4096,768]{1,0:T(8,128)(2,1)} async-done(((bf16[512,768]{1,0:T(8,128)(2,1)}), bf16[4096,768]{1,0:T(8,128)(2,1)}) %all-gather.17.cloned.1.call-update) | async-done | bytes 6291472 | tf_op jit(solution)/shard_map/all_gather | solution.py:125
  243.5 47.3 %all-gather.13.cloned.1.call-done = bf16[4096,768]{1,0:T(8,128)(2,1)} async-done(((bf16[512,768]{1,0:T(8,128)(2,1)}), bf16[4096,768]{1,0:T(8,128)(2,1)}) %all-gather.13.cloned.1.call-update) | async-done | bytes 6291472 | tf_op jit(solution)/shard_map/all_gather | solution.py:126
  290.8 134.3 %while.15 = (s32[]{:T(128)}, f32[512,768]{0,1:T(8,128)}, f32[512,12]{0,1:T(8,128)}, bf16[4,1024,768]{2,1,0:T(8,128)(2,1)}, s32[4]{0:T(128)S(1)}, /*index=5*/s32[...) while((s32[]{:T(128)}, f32[512,768]{0,1:T(8,128)}, ...), condition=%wide.region_8.9_spmd.clone.clone.clone, body=%wide.region_6.8_spmd.clone.clone.clone.sunk | while | flops 1649682944 | bytes 87601416 | solution.py:137
  296.9 13.0 %fusion.52 = (f32[12,512]{1,0:T(8,128)S(1)}, f32[12,1024,512]{2,1,0:T(8,128)}) fusion(pred[512,1024]{0,1:T(8,128)(4,1)} %broadcast_compare_fusion.4, bf16[1024,12,64]{0,2,1:T(8,128)(2,1)} %bitcast.67, bf16[512,12,64]{0,2,1:T(8,128)(2,1)} %get-tuple-element.289), kind=kOutput, calls=%fused_computation.2.clone.1 | convolution fusion | flops 824174592 | bytes 28073984 | tf_op jit(solution)/shard_map/while/body/eval_jaxpr/qhd,khd->hqk/dot_general | solution.py:102
  311.5 11.7 %fusion.53 = f32[12,64,512]{2,1,0:T(8,128)S(1)} fusion(bf16[1024,12,64]{0,2,1:T(8,128)(2,1)} %bitcast.68, f32[12,1024,512]{2,1,0:T(8,128)} %get-tuple-element.258, pred[512,1024]{0,1:T(8,128)(4,1)} %broadcast_compare_fusion.4), kind=kOutput, calls=%fused_computation.4.clone.1 | convolution fusion | flops 824180736 | bytes 28835840 | tf_op jit(solution)/shard_map/while/body/eval_jaxpr/hqk,khd->qhd/dot_general | solution.py:113
  331.1 13.0 %fusion.52 = (f32[12,512]{1,0:T(8,128)S(1)}, f32[12,1024,512]{2,1,0:T(8,128)}) fusion(pred[512,1024]{0,1:T(8,128)(4,1)} %broadcast_compare_fusion.4, bf16[1024,12,64]{0,2,1:T(8,128)(2,1)} %bitcast.67, bf16[512,12,64]{0,2,1:T(8,128)(2,1)} %get-tuple-element.289), kind=kOutput, calls=%fused_computation.2.clone.1 | convolution fusion | flops 824174592 | bytes 28073984 | tf_op jit(solution)/shard_map/while/body/eval_jaxpr/qhd,khd->hqk/dot_general | solution.py:102
  345.7 10.9 %fusion.53 = f32[12,64,512]{2,1,0:T(8,128)S(1)} fusion(bf16[1024,12,64]{0,2,1:T(8,128)(2,1)} %bitcast.68, f32[12,1024,512]{2,1,0:T(8,128)} %get-tuple-element.258, pred[512,1024]{0,1:T(8,128)(4,1)} %broadcast_compare_fusion.4), kind=kOutput, calls=%fused_computation.4.clone.1 | convolution fusion | flops 824180736 | bytes 28835840 | tf_op jit(solution)/shard_map/while/body/eval_jaxpr/hqk,khd->qhd/dot_general | solution.py:113
  364.5 13.0 %fusion.52 = (f32[12,512]{1,0:T(8,128)S(1)}, f32[12,1024,512]{2,1,0:T(8,128)}) fusion(pred[512,1024]{0,1:T(8,128)(4,1)} %broadcast_compare_fusion.4, bf16[1024,12,64]{0,2,1:T(8,128)(2,1)} %bitcast.67, bf16[512,12,64]{0,2,1:T(8,128)(2,1)} %get-tuple-element.289), kind=kOutput, calls=%fused_computation.2.clone.1 | convolution fusion | flops 824174592 | bytes 28073984 | tf_op jit(solution)/shard_map/while/body/eval_jaxpr/qhd,khd->hqk/dot_general | solution.py:102
  379.1 10.9 %fusion.53 = f32[12,64,512]{2,1,0:T(8,128)S(1)} fusion(bf16[1024,12,64]{0,2,1:T(8,128)(2,1)} %bitcast.68, f32[12,1024,512]{2,1,0:T(8,128)} %get-tuple-element.258, pred[512,1024]{0,1:T(8,128)(4,1)} %broadcast_compare_fusion.4), kind=kOutput, calls=%fused_computation.4.clone.1 | convolution fusion | flops 824180736 | bytes 28835840 | tf_op jit(solution)/shard_map/while/body/eval_jaxpr/hqk,khd->qhd/dot_general | solution.py:113
  397.8 13.0 %fusion.52 = (f32[12,512]{1,0:T(8,128)S(1)}, f32[12,1024,512]{2,1,0:T(8,128)}) fusion(pred[512,1024]{0,1:T(8,128)(4,1)} %broadcast_compare_fusion.4, bf16[1024,12,64]{0,2,1:T(8,128)(2,1)} %bitcast.67, bf16[512,12,64]{0,2,1:T(8,128)(2,1)} %get-tuple-element.289), kind=kOutput, calls=%fused_computation.2.clone.1 | convolution fusion | flops 824174592 | bytes 28073984 | tf_op jit(solution)/shard_map/while/body/eval_jaxpr/qhd,khd->hqk/dot_general | solution.py:102
  412.4 10.9 %fusion.53 = f32[12,64,512]{2,1,0:T(8,128)S(1)} fusion(bf16[1024,12,64]{0,2,1:T(8,128)(2,1)} %bitcast.68, f32[12,1024,512]{2,1,0:T(8,128)} %get-tuple-element.258, pred[512,1024]{0,1:T(8,128)(4,1)} %broadcast_compare_fusion.4), kind=kOutput, calls=%fused_computation.4.clone.1 | convolution fusion | flops 824180736 | bytes 28835840 | tf_op jit(solution)/shard_map/while/body/eval_jaxpr/hqk,khd->qhd/dot_general | solution.py:113
  425.0 2.5 fusion.18
  428.6 62.7 %all-gather.21.cloned.1.call-done = bf16[512,3072]{0,1:T(8,128)(2,1)} async-done(((bf16[512,768]{0,1:T(8,128)(2,1)}), bf16[512,3072]{0,1:T(8,128)(2,1)}) %all-gather.21.cloned.1.call-update) | async-done | bytes 3145744 | tf_op jit(solution)/shard_map/all_gather | solution.py:152
  491.3 6.9 %add_convert_fusion = bf16[512,768]{1,0:T(8,128)(2,1)} fusion(bf16[512,768]{1,0:T(8,128)(2,1)S(1)} %copy-done.7, bf16[512,3072]{0,1:T(8,128)(2,1)} %all-gather.21.cloned.1.call-done, bf16[3072,768]{1,0:T(8,128)(2,1)} %all-gather.23.cloned.1.call-done, f32[768]{0:T(1024)S(1)} %get-tuple-element.157, f32[768]{0:T(1024)S(1)} %get-tuple-element.156, ...), kind=kOutput, calls=%fused_computation.30 | convolution fusion | flops 2417885184 | bytes 9443840 | tf_op jit(solution)/shard_map/dot_general | solution.py:155
  (158 shorter events, 57.6 us)
Async XLA Ops:
  6.5 2.9 copy-start.17
  6.5 2.9 copy-start.21
  6.5 3.0 copy-start.22
  6.5 4.1 copy-start.16
  6.5 68.6 %all-gather.9.cloned.1.call-start = ((), (), s32[]{:S(2)}) async-start(), calls=%async_computation | async-start | bytes 3932160 | tf_op jit(solution)/shard_map/all_gather | solution.py:76
  7.3 107.4 %all-gather.15.cloned.1.call-start = ((), (), s32[]{:S(2)}) async-start(), calls=%async_computation.3 | async-start | bytes 5308416 | tf_op jit(solution)/shard_map/all_gather | solution.py:83
  8.0 147.5 %all-gather.19.cloned.1.call-start = ((), (), s32[]{:S(2)}) async-start(), calls=%async_computation.5 | async-start | bytes 5308416 | tf_op jit(solution)/shard_map/all_gather | solution.py:82
  8.8 187.4 %all-gather.11.cloned.1.call-start = ((), (), s32[]{:S(2)}) async-start(), calls=%async_computation.1 | async-start | bytes 5308416 | tf_op jit(solution)/shard_map/all_gather | solution.py:84
  9.3 234.1 %all-gather.17.cloned.1.call-start = ((), (), s32[]{:S(2)}) async-start(), calls=%async_computation.4 | async-start | bytes 7077888 | tf_op jit(solution)/shard_map/all_gather | solution.py:125
  9.6 194.2 %copy-start.18 = (pred[512]{0:T(512)(128)(4,1)}, pred[512]{0:T(512)(128)(4,1)S(1)}, u32[]{:S(2)}) copy-start(pred[512]{0:T(512)(128)(4,1)S(1)} %subtract_compare_fusion) | copy-start | bytes 1540
  75.1 2.8 copy-start.2
  174.9 28.9 %copy-start.9 = (f32[512,12]{0,1:T(8,128)S(1)}, f32[512,12]{0,1:T(8,128)}, u32[]{:S(2)}) copy-start(f32[512,12]{0,1:T(8,128)} %copy-done.8) | copy-start | bytes 73732
  174.9 28.9 %copy-start.12 = (f32[512,12]{0,1:T(8,128)S(1)}, f32[512,12]{0,1:T(8,128)}, u32[]{:S(2)}) copy-start(f32[512,12]{0,1:T(8,128)} %copy-done.11) | copy-start | bytes 73732
  174.9 115.9 %all-gather.13.cloned.1.call-start = ((), (), s32[]{:S(2)}) async-start(), calls=%async_computation.2 | async-start | bytes 7077888 | tf_op jit(solution)/shard_map/all_gather | solution.py:126
  203.0 225.6 %all-gather.23.cloned.1.call-start = ((), (), s32[]{:S(2)}) async-start(), calls=%async_computation.7 | async-start | bytes 5308416 | tf_op jit(solution)/shard_map/all_gather | solution.py:157
  203.7 287.5 %all-gather.21.cloned.1.call-start = ((), (), s32[]{:S(2)}) async-start(), calls=%async_computation.6 | async-start | bytes 3932160 | tf_op jit(solution)/shard_map/all_gather | solution.py:152
  311.5 11.7 %copy-start = (f32[512,768]{0,1:T(8,128)S(1)}, f32[512,768]{0,1:T(8,128)}, u32[]{:S(2)}) copy-start(f32[512,768]{0,1:T(8,128)} %get-tuple-element.272) | copy-start | bytes 4718596 | tf_op jit(solution)/shard_map/while
  323.7 1.2 copy-start.1
  345.7 10.9 %copy-start = (f32[512,768]{0,1:T(8,128)S(1)}, f32[512,768]{0,1:T(8,128)}, u32[]{:S(2)}) copy-start(f32[512,768]{0,1:T(8,128)} %get-tuple-element.272) | copy-start | bytes 4718596 | tf_op jit(solution)/shard_map/while
  357.1 1.2 copy-start.1
  379.1 10.9 %copy-start = (f32[512,768]{0,1:T(8,128)S(1)}, f32[512,768]{0,1:T(8,128)}, u32[]{:S(2)}) copy-start(f32[512,768]{0,1:T(8,128)} %get-tuple-element.272) | copy-start | bytes 4718596 | tf_op jit(solution)/shard_map/while
  412.4 10.9 %copy-start = (f32[512,768]{0,1:T(8,128)S(1)}, f32[512,768]{0,1:T(8,128)}, u32[]{:S(2)}) copy-start(f32[512,768]{0,1:T(8,128)} %get-tuple-element.272) | copy-start | bytes 4718596 | tf_op jit(solution)/shard_map/while
  425.0 66.2 %copy-start.7 = (bf16[512,768]{1,0:T(8,128)(2,1)S(1)}, bf16[512,768]{1,0:T(8,128)(2,1)}, u32[]{:S(2)}) copy-start(bf16[512,768]{1,0:T(8,128)(2,1)} %param.12) | copy-start | bytes 2359300
  425.0 66.2 %copy-start.19 = (pred[512]{0:T(512)(128)(4,1)S(1)}, pred[512]{0:T(512)(128)(4,1)}, u32[]{:S(2)}) copy-start(pred[512]{0:T(512)(128)(4,1)} %copy-done.18) | copy-start | bytes 1540
  (19 other events, 16.2 us)
Sparse Core Ops, SparseCore 0:
  8.9 66.1 all-gather.8
  77.0 37.5 all-gather.14
  116.5 38.9 all-gather.18
  157.2 38.9 all-gather.10
  197.9 45.5 all-gather.16
  245.2 45.5 all-gather.12
  292.7 38.9 all-gather.22
  427.7 63.4 all-gather.20
where the time goes:
time: 506 us; the launch traced here: 505 us
  waiting for transfers between devices  303 us (60%)
  matrix products  121 us (24%)
  local copies, waits for them, and re-layouts  38.3 us (8%)
  other arithmetic  28 us (6%)
  between operations  13.9 us (3%)
    all_gather x1, waiting for transfers between devices, shards(): full_rows = lax.all_gather(hidden_states, 'mdl', axis=1, tiled=True)  64.5 us
    all_gather x1, waiting for transfers between devices, shards(): all_heads = lax.all_gather(attended, 'mdl', axis=1, tiled=True)  62.7 us
    dot_general x4, matrix products, block_terms(): jnp.einsum('qhd,khd->hqk', query, block_keys.reshape(size, local_heads, h...  51.9 us
    all_gather x1, waiting for transfers between devices, shards(): values_piece = lax.all_gather(value_flat, 'tok', axis=0, tiled=True)  47.3 us
    dot_general x4, matrix products, block_terms(): jnp.einsum('hqk,khd->qhd', expo.astype(jnp.bfloat16), block_values.reshap...  44.4 us
    all_gather x1, waiting for transfers between devices, shards(): keys_piece = lax.all_gather(key_flat, 'tok', axis=0, tiled=True)  38.2 us
    all_gather x1, waiting for transfers between devices, shards(): lax.all_gather(query_weight, 'tok', axis=0, tiled=True)  33.6 us
    all_gather x1, waiting for transfers between devices, shards(): lax.all_gather(key_weight, 'tok', axis=0, tiled=True)  32 us
  transfers between devices with their start and end apart: 8, of which 7 were waited for; matrix products, arithmetic and copies ran while one was open for 34% of the time, Pallas kernels for 0%

commit v1 on v0

--- a/solution.py
+++ b/solution.py
@@ -73,7 +73,23 @@
     local_width = query_weight.shape[1]
     head_width = query_gain.shape[0]
     local_heads = local_width // head_width
-    full_rows = lax.all_gather(hidden_states, "mdl", axis=1, tiled=True)
+
+    def stages_all_hold(x_part):
+        reply, m_next = (lax.psum(1, axis_name="mdl"), lax.axis_index("mdl"))
+        aux, f_now = (x_part, 1)
+        while f_now < reply:
+            w_next = lax.ppermute(
+                aux,
+                axis_name="mdl",
+                perm=list(map(lambda hop_no: (hop_no, hop_no ^ f_now), range(reply))),
+            )
+            local_next = jnp.concatenate([aux, w_next], axis=1)
+            all_rows = jnp.concatenate([w_next, aux], axis=1)
+            aux = jnp.where(m_next & f_now == 0, local_next, all_rows)
+            f_now = 2 * f_now
+        return aux
+
+    full_rows = stages_all_hold(hidden_states)
     row_index = lax.axis_index("tok") * own_rows + jnp.arange(own_rows, dtype=jnp.int32)
     request, is_text, bound = token_labels(row_index, lengths)
     normed = modulate(full_rows, modulation, is_text)

time: 506 us -> 443 us (0.88)
  waiting for transfers between devices: 303 us -> 233 us
  starting transfers between devices: 0.49 us -> 6.35 us
    ppermute x0 -> x2, waiting for transfers between devices: none -> 84 us  [stages_all_hold(): lax.ppermute(aux, axis_name='mdl', perm=list(map(lambda hop_no: (hop_no,...]
    all_gather x1 -> x0, waiting for transfers between devices: 64.5 us -> none  [shards(): full_rows = lax.all_gather(hidden_states, 'mdl', axis=1, tiled=True)]
    all_gather x1, waiting for transfers between devices: 33.6 us -> 0.01 us  [shards(): lax.all_gather(query_weight, 'tok', axis=0, tiled=True)]
    all_gather x1, waiting for transfers between devices: 32 us -> 0.01 us  [shards(): lax.all_gather(key_weight, 'tok', axis=0, tiled=True)]
    all_gather x1, waiting for transfers between devices: 21 us -> 0.02 us  [shards(): lax.all_gather(value_weight, 'tok', axis=0, tiled=True)]
    ppermute x0 -> x2, starting transfers between devices: none -> 5.9 us  [stages_all_hold(): lax.ppermute(aux, axis_name='mdl', perm=list(map(lambda hop_no: (hop_no,...]
  transfers between devices with their start and end apart: 8 -> 9, of which waited for: 7 -> 5; matrix products, arithmetic and copies ran while one was open for 34% -> 40% of each run, Pallas kernels for 0% -> 0%
where the time goes in v1:
time: 443 us; the launch traced here: 442 us
  waiting for transfers between devices  233 us (53%)
  matrix products  122 us (28%)
  local copies, waits for them, and re-layouts  36.9 us (8%)
  other arithmetic  29.5 us (7%)
  between operations  13.9 us (3%)
  starting transfers between devices  6.35 us (1%)
    ppermute x2, waiting for transfers between devices, stages_all_hold(): lax.ppermute(aux, axis_name='mdl', perm=list(map(lambda hop_no: (hop_no,...  84 us
    all_gather x1, waiting for transfers between devices, shards(): all_heads = lax.all_gather(attended, 'mdl', axis=1, tiled=True)  62.7 us
    dot_general x4, matrix products, block_terms(): jnp.einsum('qhd,khd->hqk', query, block_keys.reshape(size, local_heads, h...  51.9 us
    all_gather x1, waiting for transfers between devices, shards(): values_piece = lax.all_gather(value_flat, 'tok', axis=0, tiled=True)  47.3 us
    dot_general x4, matrix products, block_terms(): jnp.einsum('hqk,khd->qhd', expo.astype(jnp.bfloat16), block_values.reshap...  44.4 us
    all_gather x1, waiting for transfers between devices, shards(): keys_piece = lax.all_gather(key_flat, 'tok', axis=0, tiled=True)  37.4 us
    dynamic_slice x16, local copies, waits for them, and re-layouts, shards(): lax.scan(step_block, initial, (keys_piece.reshape(steps_count, block, loc...  23.7 us
    dot_general x3, matrix products, shards(): jnp.dot(columns, pieces[number], preferred_element_type=jnp.float32)  18.9 us
  transfers between devices with their start and end apart: 9, of which 5 were waited for; matrix products, arithmetic and copies ran while one was open for 40% of the time, Pallas kernels for 0%

profile of v1, /device:TPU:0, one launch (start us, length us, event | category | flops | bytes accessed | tf_op | source)
XLA Modules:
  0.0 442.4 jit_solution(3644226987056116571)
XLA Ops:
  8.1 3.1 collective-permute-start
  11.2 17.7 %collective-permute-done = bf16[512,768]{1,0:T(8,128)(2,1)S(1)} collective-permute-done((bf16[512,768]{1,0:T(8,128)(2,1)}, bf16[512,768]{1,0:T(8,128)(2,1)S(1)}, u32[]{:S(2)}, u32[]{:S(2)}) %collective-permute-start) | collective-permute-done | bytes 786464 | tf_op jit(solution)/shard_map/ppermute | solution.py:81
  30.8 2.8 collective-permute-start.1
  34.8 66.3 %collective-permute-done.1 = bf16[512,1536]{1,0:T(8,128)(2,1)S(1)} collective-permute-done((bf16[512,1536]{1,0:T(8,128)(2,1)S(1)}, bf16[512,1536]{1,0:T(8,128)(2,1)S(1)}, u32[]{:S(2)}, u32[]{:S(2)}) %collective-permute-start.1) | collective-permute-done | bytes 1572896 | tf_op jit(solution)/shard_map/ppermute | solution.py:81
  103.7 4.1 fusion.16
  107.9 5.9 %fusion.25 = f32[512,768]{1,0:T(8,128)S(1)} fusion(bf16[512,3072]{1,0:T(8,128)(2,1)} %fusion.16, bf16[3072,768]{1,0:T(8,128)(2,1)} %all-gather.12.cloned.1.call-done), kind=kOutput, calls=%fused_computation.66 | convolution fusion | flops 2415919104 | bytes 9437184 | tf_op jit(solution)/shard_map/dot_general | solution.py:105
  114.9 6.3 %fusion.26 = f32[512,768]{0,1:T(8,128)S(1)} fusion(bf16[512,3072]{1,0:T(8,128)(2,1)} %fusion.16, bf16[3072,768]{1,0:T(8,128)(2,1)} %all-gather.16.cloned.1.call-done), kind=kOutput, calls=%fused_computation.67 | convolution fusion | flops 2415919104 | bytes 9437184 | tf_op jit(solution)/shard_map/dot_general | solution.py:105
  130.7 3.9 select_convert_fusion
  134.8 6.8 %convolution_convert_fusion = bf16[512,768]{1,0:T(8,128)(2,1)} fusion(bf16[512,3072]{1,0:T(8,128)(2,1)} %fusion.16, bf16[3072,768]{1,0:T(8,128)(2,1)} %all-gather.8.cloned.1.call-done), kind=kOutput, calls=%fused_computation.38 | convolution fusion | flops 2416312320 | bytes 8650752 | tf_op jit(solution)/shard_map/dot_general | solution.py:105
  143.7 37.4 %all-gather.14.cloned.1.call-done = bf16[4096,768]{1,0:T(8,128)(2,1)} async-done(((bf16[512,768]{1,0:T(8,128)(2,1)}), bf16[4096,768]{1,0:T(8,128)(2,1)}) %all-gather.14.cloned.1.call-update) | async-done | bytes 6291472 | tf_op jit(solution)/shard_map/all_gather | solution.py:141
  181.0 47.3 %all-gather.10.cloned.1.call-done = bf16[4096,768]{1,0:T(8,128)(2,1)} async-done(((bf16[512,768]{1,0:T(8,128)(2,1)}), bf16[4096,768]{1,0:T(8,128)(2,1)}) %all-gather.10.cloned.1.call-update) | async-done | bytes 6291472 | tf_op jit(solution)/shard_map/all_gather | solution.py:142
  228.3 134.2 %while.15 = (s32[]{:T(128)}, f32[512,768]{0,1:T(8,128)}, f32[512,12]{0,1:T(8,128)}, bf16[4,1024,768]{2,1,0:T(8,128)(2,1)}, s32[4]{0:T(128)S(1)}, /*index=5*/s32[...) while((s32[]{:T(128)}, f32[512,768]{0,1:T(8,128)}, ...), condition=%wide.region_8.9_spmd.clone.clone.clone, body=%wide.region_6.8_spmd.clone.clone.clone.sunk | while | flops 1649682944 | bytes 87601416 | solution.py:153
  234.4 13.0 %fusion.52 = (f32[12,512]{1,0:T(8,128)S(1)}, f32[12,1024,512]{2,1,0:T(8,128)}) fusion(pred[512,1024]{0,1:T(8,128)(4,1)} %broadcast_compare_fusion.4, bf16[1024,12,64]{0,2,1:T(8,128)(2,1)} %bitcast.67, bf16[512,12,64]{0,2,1:T(8,128)(2,1)} %get-tuple-element.289), kind=kOutput, calls=%fused_computation.2.clone.1 | convolution fusion | flops 824174592 | bytes 28073984 | tf_op jit(solution)/shard_map/while/body/eval_jaxpr/qhd,khd->hqk/dot_general | solution.py:118
  249.0 11.7 %fusion.53 = f32[12,64,512]{2,1,0:T(8,128)S(1)} fusion(bf16[1024,12,64]{0,2,1:T(8,128)(2,1)} %bitcast.68, f32[12,1024,512]{2,1,0:T(8,128)} %get-tuple-element.258, pred[512,1024]{0,1:T(8,128)(4,1)} %broadcast_compare_fusion.4), kind=kOutput, calls=%fused_computation.4.clone.1 | convolution fusion | flops 824180736 | bytes 28835840 | tf_op jit(solution)/shard_map/while/body/eval_jaxpr/hqk,khd->qhd/dot_general | solution.py:129
  268.6 13.0 %fusion.52 = (f32[12,512]{1,0:T(8,128)S(1)}, f32[12,1024,512]{2,1,0:T(8,128)}) fusion(pred[512,1024]{0,1:T(8,128)(4,1)} %broadcast_compare_fusion.4, bf16[1024,12,64]{0,2,1:T(8,128)(2,1)} %bitcast.67, bf16[512,12,64]{0,2,1:T(8,128)(2,1)} %get-tuple-element.289), kind=kOutput, calls=%fused_computation.2.clone.1 | convolution fusion | flops 824174592 | bytes 28073984 | tf_op jit(solution)/shard_map/while/body/eval_jaxpr/qhd,khd->hqk/dot_general | solution.py:118
  283.2 10.9 %fusion.53 = f32[12,64,512]{2,1,0:T(8,128)S(1)} fusion(bf16[1024,12,64]{0,2,1:T(8,128)(2,1)} %bitcast.68, f32[12,1024,512]{2,1,0:T(8,128)} %get-tuple-element.258, pred[512,1024]{0,1:T(8,128)(4,1)} %broadcast_compare_fusion.4), kind=kOutput, calls=%fused_computation.4.clone.1 | convolution fusion | flops 824180736 | bytes 28835840 | tf_op jit(solution)/shard_map/while/body/eval_jaxpr/hqk,khd->qhd/dot_general | solution.py:129
  298.2 2.1 constant_dynamic-slice_fusion.3
  301.9 13.0 %fusion.52 = (f32[12,512]{1,0:T(8,128)S(1)}, f32[12,1024,512]{2,1,0:T(8,128)}) fusion(pred[512,1024]{0,1:T(8,128)(4,1)} %broadcast_compare_fusion.4, bf16[1024,12,64]{0,2,1:T(8,128)(2,1)} %bitcast.67, bf16[512,12,64]{0,2,1:T(8,128)(2,1)} %get-tuple-element.289), kind=kOutput, calls=%fused_computation.2.clone.1 | convolution fusion | flops 824174592 | bytes 28073984 | tf_op jit(solution)/shard_map/while/body/eval_jaxpr/qhd,khd->hqk/dot_general | solution.py:118
  316.5 10.9 %fusion.53 = f32[12,64,512]{2,1,0:T(8,128)S(1)} fusion(bf16[1024,12,64]{0,2,1:T(8,128)(2,1)} %bitcast.68, f32[12,1024,512]{2,1,0:T(8,128)} %get-tuple-element.258, pred[512,1024]{0,1:T(8,128)(4,1)} %broadcast_compare_fusion.4), kind=kOutput, calls=%fused_computation.4.clone.1 | convolution fusion | flops 824180736 | bytes 28835840 | tf_op jit(solution)/shard_map/while/body/eval_jaxpr/hqk,khd->qhd/dot_general | solution.py:129
  335.3 13.0 %fusion.52 = (f32[12,512]{1,0:T(8,128)S(1)}, f32[12,1024,512]{2,1,0:T(8,128)}) fusion(pred[512,1024]{0,1:T(8,128)(4,1)} %broadcast_compare_fusion.4, bf16[1024,12,64]{0,2,1:T(8,128)(2,1)} %bitcast.67, bf16[512,12,64]{0,2,1:T(8,128)(2,1)} %get-tuple-element.289), kind=kOutput, calls=%fused_computation.2.clone.1 | convolution fusion | flops 824174592 | bytes 28073984 | tf_op jit(solution)/shard_map/while/body/eval_jaxpr/qhd,khd->hqk/dot_general | solution.py:118
  349.9 10.9 %fusion.53 = f32[12,64,512]{2,1,0:T(8,128)S(1)} fusion(bf16[1024,12,64]{0,2,1:T(8,128)(2,1)} %bitcast.68, f32[12,1024,512]{2,1,0:T(8,128)} %get-tuple-element.258, pred[512,1024]{0,1:T(8,128)(4,1)} %broadcast_compare_fusion.4), kind=kOutput, calls=%fused_computation.4.clone.1 | convolution fusion | flops 824180736 | bytes 28835840 | tf_op jit(solution)/shard_map/while/body/eval_jaxpr/hqk,khd->qhd/dot_general | solution.py:129
  362.5 2.5 fusion.18
  366.0 62.7 %all-gather.18.cloned.1.call-done = bf16[512,3072]{0,1:T(8,128)(2,1)} async-done(((bf16[512,768]{0,1:T(8,128)(2,1)}), bf16[512,3072]{0,1:T(8,128)(2,1)}) %all-gather.18.cloned.1.call-update) | async-done | bytes 3145744 | tf_op jit(solution)/shard_map/all_gather | solution.py:168
  428.7 6.9 %add_convert_fusion = bf16[512,768]{1,0:T(8,128)(2,1)} fusion(bf16[512,768]{1,0:T(8,128)(2,1)S(1)} %copy-done.6, bf16[512,3072]{0,1:T(8,128)(2,1)} %all-gather.18.cloned.1.call-done, bf16[3072,768]{1,0:T(8,128)(2,1)} %all-gather.20.cloned.1.call-done, f32[768]{0:T(1024)S(1)} %get-tuple-element.157, f32[768]{0:T(1024)S(1)} %get-tuple-element.156, ...), kind=kOutput, calls=%fused_computation.32 | convolution fusion | flops 2417885184 | bytes 9443840 | tf_op jit(solution)/shard_map/dot_general | solution.py:171
  (158 shorter events, 56.3 us)
Async XLA Ops:
  6.5 27.0 %copy-start.16 = (s32[3,512]{1,0:T(4,128)S(1)}, s32[3,512]{1,0:T(4,128)}, u32[]{:S(2)}) copy-start(s32[3,512]{1,0:T(4,128)} %param.14) | copy-start | bytes 18436
  6.5 27.0 %copy-start.20 = (f32[64]{0:T(128)S(1)}, f32[64]{0:T(128)}, u32[]{:S(2)}) copy-start(f32[64]{0:T(128)} %param.21) | copy-start | bytes 772
  6.5 27.1 %copy-start.21 = (s32[2]{0:T(128)S(1)}, s32[2]{0:T(128)}, u32[]{:S(2)}) copy-start(s32[2]{0:T(128)} %param.13) | copy-start | bytes 28
  6.5 28.2 %copy-start.15 = (f32[6,3072]{1,0:T(8,128)S(1)}, f32[6,3072]{1,0:T(8,128)}, u32[]{:S(2)}) copy-start(f32[6,3072]{1,0:T(8,128)} %param.15) | copy-start | bytes 221188
  6.5 101.3 %all-gather.12.cloned.1.call-start = ((), (), s32[]{:S(2)}) async-start(), calls=%async_computation.2 | async-start | bytes 5308416 | tf_op jit(solution)/shard_map/all_gather | solution.py:99
  7.3 107.6 %all-gather.16.cloned.1.call-start = ((), (), s32[]{:S(2)}) async-start(), calls=%async_computation.4 | async-start | bytes 5308416 | tf_op jit(solution)/shard_map/all_gather | solution.py:98
  8.0 126.8 %all-gather.8.cloned.1.call-start = ((), (), s32[]{:S(2)}) async-start(), calls=%async_computation | async-start | bytes 5308416 | tf_op jit(solution)/shard_map/all_gather | solution.py:100
  8.1 20.8 %collective-permute-start = (bf16[512,768]{1,0:T(8,128)(2,1)}, bf16[512,768]{1,0:T(8,128)(2,1)S(1)}, u32[]{:S(2)}, u32[]{:S(2)}) collective-permute-start(bf16[512,768]{1,0:T(8,128)(2,1)} %param.12), channel_id=1, source_target_pairs={{0,1},{1,0},{2,3},{3,2},{4,5},{5,4},{6,7},{7,6},{8,9},{9,8},{10,11... | collective-permute-start | bytes 2359304 | tf_op jit(solution)/shard_map/ppermute | solution.py:81
  11.2 169.8 %all-gather.14.cloned.1.call-start = ((), (), s32[]{:S(2)}) async-start(), calls=%async_computation.3 | async-start | bytes 7077888 | tf_op jit(solution)/shard_map/all_gather | solution.py:141
  30.8 70.4 %collective-permute-start.1 = (bf16[512,1536]{1,0:T(8,128)(2,1)S(1)}, bf16[512,1536]{1,0:T(8,128)(2,1)S(1)}, u32[]{:S(2)}, u32[]{:S(2)}) collective-permute-start(bf16[512,1536]{1,0:T(8,128)(2,1)S(1)} %maximum_select_fusion.1), channel_id=1, source_target_pairs={{0,2},{1,3},{2,0},{3,1},{4,6},{5,7},{6,4},{7,5},{8,10},{9,11},{10,... | collective-permute-start | bytes 4718600 | tf_op jit(solution)/shard_map/ppermute | solution.py:81
  33.7 108.5 %copy-start.17 = (pred[512]{0:T(512)(128)(4,1)}, pred[512]{0:T(512)(128)(4,1)S(1)}, u32[]{:S(2)}) copy-start(pred[512]{0:T(512)(128)(4,1)S(1)} %subtract_compare_fusion) | copy-start | bytes 1540
  134.6 7.8 %copy-start.3 = (bf16[512,12,32]{0,2,1:T(8,128)(2,1)S(1)}, bf16[512,12,32]{0,2,1:T(8,128)(2,1)}, u32[]{:S(2)}) copy-start(bf16[512,12,32]{0,2,1:T(8,128)(2,1)} %get-tuple-element.181) | copy-start | bytes 1179652
  134.6 7.8 %copy-start.8 = (f32[512,12]{0,1:T(8,128)S(1)}, f32[512,12]{0,1:T(8,128)}, u32[]{:S(2)}) copy-start(f32[512,12]{0,1:T(8,128)} %copy-done.7) | copy-start | bytes 73732
  134.6 7.8 %copy-start.11 = (f32[512,12]{0,1:T(8,128)S(1)}, f32[512,12]{0,1:T(8,128)}, u32[]{:S(2)}) copy-start(f32[512,12]{0,1:T(8,128)} %copy-done.10) | copy-start | bytes 73732
  134.6 93.7 %all-gather.10.cloned.1.call-start = ((), (), s32[]{:S(2)}) async-start(), calls=%async_computation.1 | async-start | bytes 7077888 | tf_op jit(solution)/shard_map/all_gather | solution.py:142
  141.6 224.3 %all-gather.20.cloned.1.call-start = ((), (), s32[]{:S(2)}) async-start(), calls=%async_computation.6 | async-start | bytes 5308416 | tf_op jit(solution)/shard_map/all_gather | solution.py:173
  142.2 286.5 %all-gather.18.cloned.1.call-start = ((), (), s32[]{:S(2)}) async-start(), calls=%async_computation.5 | async-start | bytes 3932160 | tf_op jit(solution)/shard_map/all_gather | solution.py:168
  249.0 11.7 %copy-start = (f32[512,768]{0,1:T(8,128)S(1)}, f32[512,768]{0,1:T(8,128)}, u32[]{:S(2)}) copy-start(f32[512,768]{0,1:T(8,128)} %get-tuple-element.272) | copy-start | bytes 4718596 | tf_op jit(solution)/shard_map/while
  283.2 10.9 %copy-start = (f32[512,768]{0,1:T(8,128)S(1)}, f32[512,768]{0,1:T(8,128)}, u32[]{:S(2)}) copy-start(f32[512,768]{0,1:T(8,128)} %get-tuple-element.272) | copy-start | bytes 4718596 | tf_op jit(solution)/shard_map/while
  294.6 1.2 copy-start.1
  316.5 10.9 %copy-start = (f32[512,768]{0,1:T(8,128)S(1)}, f32[512,768]{0,1:T(8,128)}, u32[]{:S(2)}) copy-start(f32[512,768]{0,1:T(8,128)} %get-tuple-element.272) | copy-start | bytes 4718596 | tf_op jit(solution)/shard_map/while
  349.9 10.9 %copy-start = (f32[512,768]{0,1:T(8,128)S(1)}, f32[512,768]{0,1:T(8,128)}, u32[]{:S(2)}) copy-start(f32[512,768]{0,1:T(8,128)} %get-tuple-element.272) | copy-start | bytes 4718596 | tf_op jit(solution)/shard_map/while
  362.5 66.2 %copy-start.6 = (bf16[512,768]{1,0:T(8,128)(2,1)S(1)}, bf16[512,768]{1,0:T(8,128)(2,1)}, u32[]{:S(2)}) copy-start(bf16[512,768]{1,0:T(8,128)(2,1)} %param.12) | copy-start | bytes 2359300
  362.5 66.2 %copy-start.18 = (pred[512]{0:T(512)(128)(4,1)S(1)}, pred[512]{0:T(512)(128)(4,1)}, u32[]{:S(2)}) copy-start(pred[512]{0:T(512)(128)(4,1)} %copy-done.17) | copy-start | bytes 1540
  (19 other events, 18.0 us)
Sparse Core Ops, SparseCore 0:
  9.3 41.6 all-gather.11
  52.8 38.9 all-gather.15
  93.6 38.9 all-gather.7
  134.7 46.2 all-gather.13
  182.7 45.5 all-gather.9
  230.0 38.9 all-gather.19
  365.1 63.4 all-gather.17
